TPU v7x, 32 devices: a whole 2x2x4 slice. The times are simulated.
32 devices in a mesh: gx: 4 (over x, core), gy: 8 (over z, y).
Axes of the slice: x: 2, y: 2, z: 4, core: 2. Of those that a mesh axis runs over, the one named last changes fastest.
Arguments:
- right_side: bfloat16 [4, 8, 8, 625, 256], P('gx', 'gy'), may hold values from -6 to 6
- inverse_blocks: bfloat16 [4, 8, 8, 625, 625], P('gx', 'gy'), may hold values from -0.2 to 0.8
- lift_matrix: bfloat16 [625, 375], replicated, may hold values from -2 to 2
- plane_order: int32 [4, 8, 8], P('gx', 'gy'), may hold values from 0 to 7, each once within a row
- face_orient: int32 [4, 8, 8, 3], P('gx', 'gy'), may hold values from 0 to 7
Outputs:
- solution: bfloat16 [4, 8, 8, 625, 256], P('gx', 'gy')
Inputs may be any that keep to these rules, and one draw needn't show every extreme that they name: `plane_order`: each slab's row lists the storage slots of its 8 elements from lowest to highest z, each slot once. `face_orient`: any of the eight orientations of a square face.
All inputs are finite; a program needn't handle non-finite values.
Results may differ from a plain program's by a relative error of at most 0.025.
Values may be sent and summed in bfloat16 or wider, within the bound.
A program may use at most 64 MiB of HBM per device.

v0:
```python
import jax
import jax.numpy as jnp
import numpy as np
from jax import lax
from jax.sharding import PartitionSpec as P

VARS = 5
NODES = 5
FACE = 125
PLANES = 8


def from_behind(block, axis, distance):
    devices = range(lax.axis_size(axis))
    route = [(i - distance, i) for i in devices if i - distance in devices]
    return lax.ppermute(block, axis, route)


def orient_table():
    lookup_table = np.zeros((8, FACE), np.int32)
    for orient in range(8):
        for variable in range(VARS):
            for first in range(NODES):
                for second in range(NODES):
                    if orient & 1:
                        first_new, second_new = (second, first)
                    else:
                        first_new, second_new = (first, second)
                    if orient & 2:
                        first_new = NODES - 1 - first_new
                    if orient & 4:
                        second_new = NODES - 1 - second_new
                    target = variable * NODES * NODES + first * NODES + second
                    lookup_table[orient, target] = (
                        variable * NODES * NODES + first_new * NODES + second_new
                    )
    return lookup_table


def select_matrices(orients):
    lookup = jnp.asarray(orient_table())
    codes = jnp.arange(8, dtype=jnp.int32)[:, None]
    chosen = jnp.sum(jnp.where(orients[..., None, None] == codes, lookup, 0), axis=-2)
    return (chosen[..., None] == jnp.arange(FACE, dtype=jnp.int32)).astype(jnp.bfloat16)


def face_traces(block):
    leading = block.shape[:-2]
    columns = block.shape[-1]
    shaped = block.reshape(leading + (VARS, NODES, NODES, NODES, columns))
    along_x = shaped[..., :, NODES - 1, :, :, :].reshape(leading + (FACE, columns))
    along_y = shaped[..., :, :, NODES - 1, :, :].reshape(leading + (FACE, columns))
    along_z = shaped[..., :, :, :, NODES - 1, :].reshape(leading + (FACE, columns))
    return jnp.stack([along_x, along_y, along_z], axis=-3)


def receive(x_out, y_out):
    x_in = from_behind(x_out, "gx", 1)
    y_in = from_behind(y_out, "gy", 1)
    return (x_in, y_in)


def on_device(right_side, inverse_blocks, lift_matrix, plane_order, face_orient):
    sources = right_side[0, 0]
    blocks_all = inverse_blocks[0, 0]
    order_row = plane_order[0, 0]
    orient_all = face_orient[0, 0]
    count_x = lax.axis_size("gx")
    count_y = lax.axis_size("gy")
    place_x = lax.axis_index("gx")
    place_y = lax.axis_index("gy")
    group = 1
    num_groups = PLANES // group
    columns = sources.shape[-1]
    plane_ids = jnp.arange(PLANES, dtype=jnp.int32)
    total_steps = count_x + count_y + num_groups - 2

    def slot_of(plane):
        return jnp.sum(jnp.where(plane_ids == plane, order_row, 0))

    def source_for(slot_id, incoming):
        orients = lax.dynamic_index_in_dim(orient_all, slot_id, 0, keepdims=False)
        select = select_matrices(orients)
        turned = jnp.einsum("dqc,dcn->dqn", select, incoming, preferred_element_type=jnp.float32)
        turned = turned.astype(jnp.bfloat16).reshape(3 * FACE, columns)
        rows = lax.dynamic_index_in_dim(sources, slot_id, 0, keepdims=False)
        lifted = jnp.dot(lift_matrix, turned, preferred_element_type=jnp.float32)
        return (rows.astype(jnp.float32) - lifted).astype(jnp.bfloat16)

    def solve_block(slot_id, source):
        block = lax.dynamic_index_in_dim(blocks_all, slot_id, 0, keepdims=False)
        return jnp.dot(block, source, preferred_element_type=jnp.float32).astype(jnp.bfloat16)

    empty_face = jnp.zeros((group, FACE, columns), jnp.bfloat16)
    zero_trace = jnp.zeros((FACE, columns), jnp.bfloat16)
    solution = jnp.zeros(sources.shape, jnp.bfloat16)

    def advance_now(operands):
        x_in, y_in, x_out, y_out, z_trace, solution, group_id = operands
        x_list, y_list = ([], [])
        slot_id = slot_of(group_id * group + 0)
        incoming = jnp.stack([x_in[0], y_in[0], z_trace])
        source = source_for(slot_id, incoming)
        result = solve_block(slot_id, source)
        traces = face_traces(result)
        x_list.append(traces[0])
        y_list.append(traces[1])
        z_trace = traces[2]
        solution = lax.dynamic_update_index_in_dim(solution, result, slot_id, 0)
        return (jnp.stack(x_list), jnp.stack(y_list), z_trace, solution)

    def hold_now(operands):
        x_in, y_in, x_out, y_out, z_trace, solution, group_id = operands
        return (x_out, y_out, z_trace, solution)

    def step_now(step, carry):
        x_out, y_out, z_trace, solution = carry
        x_in, y_in = receive(x_out, y_out)
        group_id = step - place_x - place_y
        is_live = (group_id >= 0) & (group_id < num_groups)
        clipped = jnp.clip(group_id, 0, num_groups - 1)
        return lax.cond(
            is_live, advance_now, hold_now, (x_in, y_in, x_out, y_out, z_trace, solution, clipped)
        )

    final = lax.fori_loop(0, total_steps, step_now, (empty_face, empty_face, zero_trace, solution))
    solution = final[3]
    return solution[None, None]


def solution(mesh):
    placed = (
        P("gx", "gy", None, None, None),
        P("gx", "gy", None, None, None),
        P(),
        P("gx", "gy", None),
        P("gx", "gy", None, None),
    )
    return jax.shard_map(
        on_device,
        mesh=mesh,
        in_specs=placed,
        out_specs=P("gx", "gy", None, None, None),
        check_vma=False,
    )
```

profile of v0, /device:TPU:31, one launch (start us, length us, event | category | flops | bytes accessed | tf_op | source)
XLA Modules:
  0.0 268.5 jit_solution(10527647509663835083)
XLA Ops:
  0.0 1.3 copy.24
  1.3 2.0 copy.22
  3.4 3.8 %copy.32 = bf16[1,1,8,625,256]{4,3,2,1,0:T(8,128)(2,1)} copy(bf16[1,1,8,625,256]{4,2,3,1,0:T(8,128)(2,1)} %param.10) | data formatting | bytes 5120000 | tf_op args[0]
  7.1 6.4 %copy.31 = bf16[1,1,8,625,625]{4,3,2,1,0:T(8,128)(2,1)} copy(bf16[1,1,8,625,625]{4,2,3,1,0:T(8,128)(2,1)} %param.11) | data formatting | bytes 12500000 | tf_op args[1]
  13.7 252.8 %while.21 = (s32[]{:T(128)}, bf16[1,125,256]{2,1,0:T(8,128)(2,1)S(1)}, bf16[1,125,256]{2,1,0:T(8,128)(2,1)S(1)}, bf16[125,256]{1,0:T(8,128)(2,1)S(1)}, bf16[8,62...) while((s32[]{:T(128)}, ...), condition=%wide.region_5.6_spmd.clone.clone, body=%wide.region_0.5_spmd.sunk.clone.clone.sunk | while | flops 344980544 | bytes 5154825 | solution.py:126
  13.7 1.3 collective-permute-start.1
  15.0 1.3 collective-permute-start
  16.3 2.4 collective-permute-done.1
  20.0 1.3 collective-permute-start
  21.3 2.9 %collective-permute-done.1 = bf16[1,125,256]{2,1,0:T(8,128)(2,1)S(1)} collective-permute-done((bf16[1,125,256]{2,1,0:T(8,128)(2,1)S(1)}, bf16[1,125,256]{2,1,0:T(8,128)(2,1)S(1)}, u32[]{:S(2)}, u32[]{:S(2)}) %collective-permute-start.1) | collective-permute-done | bytes 64032 | tf_op jit(solution)/shard_map/while/body/eval_jaxpr/ppermute | solution.py:16
  26.5 1.3 collective-permute-start
  27.8 3.9 %collective-permute-done.1 = bf16[1,125,256]{2,1,0:T(8,128)(2,1)S(1)} collective-permute-done((bf16[1,125,256]{2,1,0:T(8,128)(2,1)S(1)}, bf16[1,125,256]{2,1,0:T(8,128)(2,1)S(1)}, u32[]{:S(2)}, u32[]{:S(2)}) %collective-permute-start.1) | collective-permute-done | bytes 64032 | tf_op jit(solution)/shard_map/while/body/eval_jaxpr/ppermute | solution.py:16
  33.4 1.3 collective-permute-start
  34.7 4.6 %collective-permute-done.1 = bf16[1,125,256]{2,1,0:T(8,128)(2,1)S(1)} collective-permute-done((bf16[1,125,256]{2,1,0:T(8,128)(2,1)S(1)}, bf16[1,125,256]{2,1,0:T(8,128)(2,1)S(1)}, u32[]{:S(2)}, u32[]{:S(2)}) %collective-permute-start.1) | collective-permute-done | bytes 64032 | tf_op jit(solution)/shard_map/while/body/eval_jaxpr/ppermute | solution.py:16
  40.8 1.3 collective-permute-start
  42.1 4.7 %collective-permute-done.1 = bf16[1,125,256]{2,1,0:T(8,128)(2,1)S(1)} collective-permute-done((bf16[1,125,256]{2,1,0:T(8,128)(2,1)S(1)}, bf16[1,125,256]{2,1,0:T(8,128)(2,1)S(1)}, u32[]{:S(2)}, u32[]{:S(2)}) %collective-permute-start.1) | collective-permute-done | bytes 64032 | tf_op jit(solution)/shard_map/while/body/eval_jaxpr/ppermute | solution.py:16
  48.3 1.3 collective-permute-start
  49.6 4.7 %collective-permute-done.1 = bf16[1,125,256]{2,1,0:T(8,128)(2,1)S(1)} collective-permute-done((bf16[1,125,256]{2,1,0:T(8,128)(2,1)S(1)}, bf16[1,125,256]{2,1,0:T(8,128)(2,1)S(1)}, u32[]{:S(2)}, u32[]{:S(2)}) %collective-permute-start.1) | collective-permute-done | bytes 64032 | tf_op jit(solution)/shard_map/while/body/eval_jaxpr/ppermute | solution.py:16
  55.8 1.3 collective-permute-start
  57.1 4.7 %collective-permute-done.1 = bf16[1,125,256]{2,1,0:T(8,128)(2,1)S(1)} collective-permute-done((bf16[1,125,256]{2,1,0:T(8,128)(2,1)S(1)}, bf16[1,125,256]{2,1,0:T(8,128)(2,1)S(1)}, u32[]{:S(2)}, u32[]{:S(2)}) %collective-permute-start.1) | collective-permute-done | bytes 64032 | tf_op jit(solution)/shard_map/while/body/eval_jaxpr/ppermute | solution.py:16
  64.6 4.7 %collective-permute-done.1 = bf16[1,125,256]{2,1,0:T(8,128)(2,1)S(1)} collective-permute-done((bf16[1,125,256]{2,1,0:T(8,128)(2,1)S(1)}, bf16[1,125,256]{2,1,0:T(8,128)(2,1)S(1)}, u32[]{:S(2)}, u32[]{:S(2)}) %collective-permute-start.1) | collective-permute-done | bytes 64032 | tf_op jit(solution)/shard_map/while/body/eval_jaxpr/ppermute | solution.py:16
  70.8 1.3 collective-permute-start
  72.1 4.7 %collective-permute-done.1 = bf16[1,125,256]{2,1,0:T(8,128)(2,1)S(1)} collective-permute-done((bf16[1,125,256]{2,1,0:T(8,128)(2,1)S(1)}, bf16[1,125,256]{2,1,0:T(8,128)(2,1)S(1)}, u32[]{:S(2)}, u32[]{:S(2)}) %collective-permute-start.1) | collective-permute-done | bytes 64032 | tf_op jit(solution)/shard_map/while/body/eval_jaxpr/ppermute | solution.py:16
  79.6 4.7 %collective-permute-done.1 = bf16[1,125,256]{2,1,0:T(8,128)(2,1)S(1)} collective-permute-done((bf16[1,125,256]{2,1,0:T(8,128)(2,1)S(1)}, bf16[1,125,256]{2,1,0:T(8,128)(2,1)S(1)}, u32[]{:S(2)}, u32[]{:S(2)}) %collective-permute-start.1) | collective-permute-done | bytes 64032 | tf_op jit(solution)/shard_map/while/body/eval_jaxpr/ppermute | solution.py:16
  85.8 1.3 collective-permute-start
  87.2 62.2 %collective-permute-done.1 = bf16[1,125,256]{2,1,0:T(8,128)(2,1)S(1)} collective-permute-done((bf16[1,125,256]{2,1,0:T(8,128)(2,1)S(1)}, bf16[1,125,256]{2,1,0:T(8,128)(2,1)S(1)}, u32[]{:S(2)}, u32[]{:S(2)}) %collective-permute-start.1) | collective-permute-done | bytes 64032 | tf_op jit(solution)/shard_map/while/body/eval_jaxpr/ppermute | solution.py:16
  149.6 8.0 %conditional.5 = ((bf16[1,125,256]{2,1,0:T(8,128)(2,1)S(1)}, bf16[1,125,256]{2,1,0:T(8,128)(2,1)S(1)}, bf16[125,256]{1,0:T(8,128)(2,1)S(1)}, bf16[8,625,256]{2,1,0:T(8,128)(2,1)S(1)})) conditional(s32[]{:T(128)} %convert_element_type.42, (bf16[1,125,256]{2,1,0:T(8,128)(2,1)S(1)}, bf16[1,125,256]{2,1,0:T(8,128)(2,1)S(1)}, ...), branch_computations={%region_1.1_spmd, %region_2.4_spmd.clone} | conditional | flops 344980544 | bytes 4642394 | solution.py:122
  149.6 1.3 fusion.17
  154.6 2.3 bitcast_dynamic-update-slice_fusion
  160.2 4.7 %collective-permute-done.1 = bf16[1,125,256]{2,1,0:T(8,128)(2,1)S(1)} collective-permute-done((bf16[1,125,256]{2,1,0:T(8,128)(2,1)S(1)}, bf16[1,125,256]{2,1,0:T(8,128)(2,1)S(1)}, u32[]{:S(2)}, u32[]{:S(2)}) %collective-permute-start.1) | collective-permute-done | bytes 64032 | tf_op jit(solution)/shard_map/while/body/eval_jaxpr/ppermute | solution.py:16
  165.1 8.0 %conditional.5 = ((bf16[1,125,256]{2,1,0:T(8,128)(2,1)S(1)}, bf16[1,125,256]{2,1,0:T(8,128)(2,1)S(1)}, bf16[125,256]{1,0:T(8,128)(2,1)S(1)}, bf16[8,625,256]{2,1,0:T(8,128)(2,1)S(1)})) conditional(s32[]{:T(128)} %convert_element_type.42, (bf16[1,125,256]{2,1,0:T(8,128)(2,1)S(1)}, bf16[1,125,256]{2,1,0:T(8,128)(2,1)S(1)}, ...), branch_computations={%region_1.1_spmd, %region_2.4_spmd.clone} | conditional | flops 344980544 | bytes 4642394 | solution.py:122
  165.1 1.3 fusion.17
  170.2 2.3 bitcast_dynamic-update-slice_fusion
  173.2 1.3 collective-permute-start.1
  174.5 1.3 collective-permute-start
  175.8 4.7 %collective-permute-done.1 = bf16[1,125,256]{2,1,0:T(8,128)(2,1)S(1)} collective-permute-done((bf16[1,125,256]{2,1,0:T(8,128)(2,1)S(1)}, bf16[1,125,256]{2,1,0:T(8,128)(2,1)S(1)}, u32[]{:S(2)}, u32[]{:S(2)}) %collective-permute-start.1) | collective-permute-done | bytes 64032 | tf_op jit(solution)/shard_map/while/body/eval_jaxpr/ppermute | solution.py:16
  180.7 8.0 %conditional.5 = ((bf16[1,125,256]{2,1,0:T(8,128)(2,1)S(1)}, bf16[1,125,256]{2,1,0:T(8,128)(2,1)S(1)}, bf16[125,256]{1,0:T(8,128)(2,1)S(1)}, bf16[8,625,256]{2,1,0:T(8,128)(2,1)S(1)})) conditional(s32[]{:T(128)} %convert_element_type.42, (bf16[1,125,256]{2,1,0:T(8,128)(2,1)S(1)}, bf16[1,125,256]{2,1,0:T(8,128)(2,1)S(1)}, ...), branch_computations={%region_1.1_spmd, %region_2.4_spmd.clone} | conditional | flops 344980544 | bytes 4642394 | solution.py:122
  180.7 1.3 fusion.17
  185.7 2.3 bitcast_dynamic-update-slice_fusion
  191.3 4.7 %collective-permute-done.1 = bf16[1,125,256]{2,1,0:T(8,128)(2,1)S(1)} collective-permute-done((bf16[1,125,256]{2,1,0:T(8,128)(2,1)S(1)}, bf16[1,125,256]{2,1,0:T(8,128)(2,1)S(1)}, u32[]{:S(2)}, u32[]{:S(2)}) %collective-permute-start.1) | collective-permute-done | bytes 64032 | tf_op jit(solution)/shard_map/while/body/eval_jaxpr/ppermute | solution.py:16
  196.2 8.0 %conditional.5 = ((bf16[1,125,256]{2,1,0:T(8,128)(2,1)S(1)}, bf16[1,125,256]{2,1,0:T(8,128)(2,1)S(1)}, bf16[125,256]{1,0:T(8,128)(2,1)S(1)}, bf16[8,625,256]{2,1,0:T(8,128)(2,1)S(1)})) conditional(s32[]{:T(128)} %convert_element_type.42, (bf16[1,125,256]{2,1,0:T(8,128)(2,1)S(1)}, bf16[1,125,256]{2,1,0:T(8,128)(2,1)S(1)}, ...), branch_computations={%region_1.1_spmd, %region_2.4_spmd.clone} | conditional | flops 344980544 | bytes 4642394 | solution.py:122
  196.2 1.3 fusion.17
  201.3 2.3 bitcast_dynamic-update-slice_fusion
  206.9 4.7 %collective-permute-done.1 = bf16[1,125,256]{2,1,0:T(8,128)(2,1)S(1)} collective-permute-done((bf16[1,125,256]{2,1,0:T(8,128)(2,1)S(1)}, bf16[1,125,256]{2,1,0:T(8,128)(2,1)S(1)}, u32[]{:S(2)}, u32[]{:S(2)}) %collective-permute-start.1) | collective-permute-done | bytes 64032 | tf_op jit(solution)/shard_map/while/body/eval_jaxpr/ppermute | solution.py:16
  211.8 8.0 %conditional.5 = ((bf16[1,125,256]{2,1,0:T(8,128)(2,1)S(1)}, bf16[1,125,256]{2,1,0:T(8,128)(2,1)S(1)}, bf16[125,256]{1,0:T(8,128)(2,1)S(1)}, bf16[8,625,256]{2,1,0:T(8,128)(2,1)S(1)})) conditional(s32[]{:T(128)} %convert_element_type.42, (bf16[1,125,256]{2,1,0:T(8,128)(2,1)S(1)}, bf16[1,125,256]{2,1,0:T(8,128)(2,1)S(1)}, ...), branch_computations={%region_1.1_spmd, %region_2.4_spmd.clone} | conditional | flops 344980544 | bytes 4642394 | solution.py:122
  211.8 1.3 fusion.17
  216.8 2.3 bitcast_dynamic-update-slice_fusion
  222.5 4.7 %collective-permute-done.1 = bf16[1,125,256]{2,1,0:T(8,128)(2,1)S(1)} collective-permute-done((bf16[1,125,256]{2,1,0:T(8,128)(2,1)S(1)}, bf16[1,125,256]{2,1,0:T(8,128)(2,1)S(1)}, u32[]{:S(2)}, u32[]{:S(2)}) %collective-permute-start.1) | collective-permute-done | bytes 64032 | tf_op jit(solution)/shard_map/while/body/eval_jaxpr/ppermute | solution.py:16
  227.4 8.0 %conditional.5 = ((bf16[1,125,256]{2,1,0:T(8,128)(2,1)S(1)}, bf16[1,125,256]{2,1,0:T(8,128)(2,1)S(1)}, bf16[125,256]{1,0:T(8,128)(2,1)S(1)}, bf16[8,625,256]{2,1,0:T(8,128)(2,1)S(1)})) conditional(s32[]{:T(128)} %convert_element_type.42, (bf16[1,125,256]{2,1,0:T(8,128)(2,1)S(1)}, bf16[1,125,256]{2,1,0:T(8,128)(2,1)S(1)}, ...), branch_computations={%region_1.1_spmd, %region_2.4_spmd.clone} | conditional | flops 344980544 | bytes 4642394 | solution.py:122
  227.4 1.3 fusion.17
  232.4 2.3 bitcast_dynamic-update-slice_fusion
  235.4 1.3 collective-permute-start.1
  236.7 1.3 collective-permute-start
  238.0 4.7 %collective-permute-done.1 = bf16[1,125,256]{2,1,0:T(8,128)(2,1)S(1)} collective-permute-done((bf16[1,125,256]{2,1,0:T(8,128)(2,1)S(1)}, bf16[1,125,256]{2,1,0:T(8,128)(2,1)S(1)}, u32[]{:S(2)}, u32[]{:S(2)}) %collective-permute-start.1) | collective-permute-done | bytes 64032 | tf_op jit(solution)/shard_map/while/body/eval_jaxpr/ppermute | solution.py:16
  242.9 8.0 %conditional.5 = ((bf16[1,125,256]{2,1,0:T(8,128)(2,1)S(1)}, bf16[1,125,256]{2,1,0:T(8,128)(2,1)S(1)}, bf16[125,256]{1,0:T(8,128)(2,1)S(1)}, bf16[8,625,256]{2,1,0:T(8,128)(2,1)S(1)})) conditional(s32[]{:T(128)} %convert_element_type.42, (bf16[1,125,256]{2,1,0:T(8,128)(2,1)S(1)}, bf16[1,125,256]{2,1,0:T(8,128)(2,1)S(1)}, ...), branch_computations={%region_1.1_spmd, %region_2.4_spmd.clone} | conditional | flops 344980544 | bytes 4642394 | solution.py:122
  242.9 1.3 fusion.17
  247.9 2.3 bitcast_dynamic-update-slice_fusion
  250.9 1.3 collective-permute-start.1
  252.2 1.3 collective-permute-start
  253.6 4.7 %collective-permute-done.1 = bf16[1,125,256]{2,1,0:T(8,128)(2,1)S(1)} collective-permute-done((bf16[1,125,256]{2,1,0:T(8,128)(2,1)S(1)}, bf16[1,125,256]{2,1,0:T(8,128)(2,1)S(1)}, u32[]{:S(2)}, u32[]{:S(2)}) %collective-permute-start.1) | collective-permute-done | bytes 64032 | tf_op jit(solution)/shard_map/while/body/eval_jaxpr/ppermute | solution.py:16
  258.5 8.0 %conditional.5 = ((bf16[1,125,256]{2,1,0:T(8,128)(2,1)S(1)}, bf16[1,125,256]{2,1,0:T(8,128)(2,1)S(1)}, bf16[125,256]{1,0:T(8,128)(2,1)S(1)}, bf16[8,625,256]{2,1,0:T(8,128)(2,1)S(1)})) conditional(s32[]{:T(128)} %convert_element_type.42, (bf16[1,125,256]{2,1,0:T(8,128)(2,1)S(1)}, bf16[1,125,256]{2,1,0:T(8,128)(2,1)S(1)}, ...), branch_computations={%region_1.1_spmd, %region_2.4_spmd.clone} | conditional | flops 344980544 | bytes 4642394 | solution.py:122
  258.5 1.3 fusion.17
  263.5 2.3 bitcast_dynamic-update-slice_fusion
  266.5 2.0 copy.33
  (166 shorter events, 50.8 us)
Async XLA Ops:
  13.7 5.0 %collective-permute-start.1 = (bf16[1,125,256]{2,1,0:T(8,128)(2,1)S(1)}, bf16[1,125,256]{2,1,0:T(8,128)(2,1)S(1)}, u32[]{:S(2)}, u32[]{:S(2)}) collective-permute-start(bf16[1,125,256]{2,1,0:T(8,128)(2,1)S(1)} %get-tuple-element.591), channel_id=1, source_target_pairs={{0,1},{1,2},{2,3},{3,4},{4,5},{5,6},{6,7},{8,9},{9,10},{10,11},{11... | collective-permute-start | bytes 192008 | tf_op jit(solution)/shard_map/while/body/eval_jaxpr/ppermute | solution.py:16
  15.0 3.7 %collective-permute-start = (bf16[1,125,256]{2,1,0:T(8,128)(2,1)S(1)}, bf16[1,125,256]{2,1,0:T(8,128)(2,1)S(1)}, u32[]{:S(2)}, u32[]{:S(2)}) collective-permute-start(bf16[1,125,256]{2,1,0:T(8,128)(2,1)S(1)} %get-tuple-element.590), channel_id=1, source_target_pairs={{0,8},{8,16},{16,24},{1,9},{9,17},{17,25},{2,10},{10,18},{18,26},{... | collective-permute-start | bytes 192008 | tf_op jit(solution)/shard_map/while/body/eval_jaxpr/ppermute | solution.py:16
  18.7 5.5 %collective-permute-start.1 = (bf16[1,125,256]{2,1,0:T(8,128)(2,1)S(1)}, bf16[1,125,256]{2,1,0:T(8,128)(2,1)S(1)}, u32[]{:S(2)}, u32[]{:S(2)}) collective-permute-start(bf16[1,125,256]{2,1,0:T(8,128)(2,1)S(1)} %get-tuple-element.591), channel_id=1, source_target_pairs={{0,1},{1,2},{2,3},{3,4},{4,5},{5,6},{6,7},{8,9},{9,10},{10,11},{11... | collective-permute-start | bytes 192008 | tf_op jit(solution)/shard_map/while/body/eval_jaxpr/ppermute | solution.py:16
  20.0 5.2 %collective-permute-start = (bf16[1,125,256]{2,1,0:T(8,128)(2,1)S(1)}, bf16[1,125,256]{2,1,0:T(8,128)(2,1)S(1)}, u32[]{:S(2)}, u32[]{:S(2)}) collective-permute-start(bf16[1,125,256]{2,1,0:T(8,128)(2,1)S(1)} %get-tuple-element.590), channel_id=1, source_target_pairs={{0,8},{8,16},{16,24},{1,9},{9,17},{17,25},{2,10},{10,18},{18,26},{... | collective-permute-start | bytes 192008 | tf_op jit(solution)/shard_map/while/body/eval_jaxpr/ppermute | solution.py:16
  25.2 6.5 %collective-permute-start.1 = (bf16[1,125,256]{2,1,0:T(8,128)(2,1)S(1)}, bf16[1,125,256]{2,1,0:T(8,128)(2,1)S(1)}, u32[]{:S(2)}, u32[]{:S(2)}) collective-permute-start(bf16[1,125,256]{2,1,0:T(8,128)(2,1)S(1)} %get-tuple-element.591), channel_id=1, source_target_pairs={{0,1},{1,2},{2,3},{3,4},{4,5},{5,6},{6,7},{8,9},{9,10},{10,11},{11... | collective-permute-start | bytes 192008 | tf_op jit(solution)/shard_map/while/body/eval_jaxpr/ppermute | solution.py:16
  26.5 5.6 %collective-permute-start = (bf16[1,125,256]{2,1,0:T(8,128)(2,1)S(1)}, bf16[1,125,256]{2,1,0:T(8,128)(2,1)S(1)}, u32[]{:S(2)}, u32[]{:S(2)}) collective-permute-start(bf16[1,125,256]{2,1,0:T(8,128)(2,1)S(1)} %get-tuple-element.590), channel_id=1, source_target_pairs={{0,8},{8,16},{16,24},{1,9},{9,17},{17,25},{2,10},{10,18},{18,26},{... | collective-permute-start | bytes 192008 | tf_op jit(solution)/shard_map/while/body/eval_jaxpr/ppermute | solution.py:16
  32.1 7.2 %collective-permute-start.1 = (bf16[1,125,256]{2,1,0:T(8,128)(2,1)S(1)}, bf16[1,125,256]{2,1,0:T(8,128)(2,1)S(1)}, u32[]{:S(2)}, u32[]{:S(2)}) collective-permute-start(bf16[1,125,256]{2,1,0:T(8,128)(2,1)S(1)} %get-tuple-element.591), channel_id=1, source_target_pairs={{0,1},{1,2},{2,3},{3,4},{4,5},{5,6},{6,7},{8,9},{9,10},{10,11},{11... | collective-permute-start | bytes 192008 | tf_op jit(solution)/shard_map/while/body/eval_jaxpr/ppermute | solution.py:16
  33.4 6.1 %collective-permute-start = (bf16[1,125,256]{2,1,0:T(8,128)(2,1)S(1)}, bf16[1,125,256]{2,1,0:T(8,128)(2,1)S(1)}, u32[]{:S(2)}, u32[]{:S(2)}) collective-permute-start(bf16[1,125,256]{2,1,0:T(8,128)(2,1)S(1)} %get-tuple-element.590), channel_id=1, source_target_pairs={{0,8},{8,16},{16,24},{1,9},{9,17},{17,25},{2,10},{10,18},{18,26},{... | collective-permute-start | bytes 192008 | tf_op jit(solution)/shard_map/while/body/eval_jaxpr/ppermute | solution.py:16
  39.5 7.3 %collective-permute-start.1 = (bf16[1,125,256]{2,1,0:T(8,128)(2,1)S(1)}, bf16[1,125,256]{2,1,0:T(8,128)(2,1)S(1)}, u32[]{:S(2)}, u32[]{:S(2)}) collective-permute-start(bf16[1,125,256]{2,1,0:T(8,128)(2,1)S(1)} %get-tuple-element.591), channel_id=1, source_target_pairs={{0,1},{1,2},{2,3},{3,4},{4,5},{5,6},{6,7},{8,9},{9,10},{10,11},{11... | collective-permute-start | bytes 192008 | tf_op jit(solution)/shard_map/while/body/eval_jaxpr/ppermute | solution.py:16
  40.8 6.2 %collective-permute-start = (bf16[1,125,256]{2,1,0:T(8,128)(2,1)S(1)}, bf16[1,125,256]{2,1,0:T(8,128)(2,1)S(1)}, u32[]{:S(2)}, u32[]{:S(2)}) collective-permute-start(bf16[1,125,256]{2,1,0:T(8,128)(2,1)S(1)} %get-tuple-element.590), channel_id=1, source_target_pairs={{0,8},{8,16},{16,24},{1,9},{9,17},{17,25},{2,10},{10,18},{18,26},{... | collective-permute-start | bytes 192008 | tf_op jit(solution)/shard_map/while/body/eval_jaxpr/ppermute | solution.py:16
  47.0 7.3 %collective-permute-start.1 = (bf16[1,125,256]{2,1,0:T(8,128)(2,1)S(1)}, bf16[1,125,256]{2,1,0:T(8,128)(2,1)S(1)}, u32[]{:S(2)}, u32[]{:S(2)}) collective-permute-start(bf16[1,125,256]{2,1,0:T(8,128)(2,1)S(1)} %get-tuple-element.591), channel_id=1, source_target_pairs={{0,1},{1,2},{2,3},{3,4},{4,5},{5,6},{6,7},{8,9},{9,10},{10,11},{11... | collective-permute-start | bytes 192008 | tf_op jit(solution)/shard_map/while/body/eval_jaxpr/ppermute | solution.py:16
  48.3 6.2 %collective-permute-start = (bf16[1,125,256]{2,1,0:T(8,128)(2,1)S(1)}, bf16[1,125,256]{2,1,0:T(8,128)(2,1)S(1)}, u32[]{:S(2)}, u32[]{:S(2)}) collective-permute-start(bf16[1,125,256]{2,1,0:T(8,128)(2,1)S(1)} %get-tuple-element.590), channel_id=1, source_target_pairs={{0,8},{8,16},{16,24},{1,9},{9,17},{17,25},{2,10},{10,18},{18,26},{... | collective-permute-start | bytes 192008 | tf_op jit(solution)/shard_map/while/body/eval_jaxpr/ppermute | solution.py:16
  54.5 7.3 %collective-permute-start.1 = (bf16[1,125,256]{2,1,0:T(8,128)(2,1)S(1)}, bf16[1,125,256]{2,1,0:T(8,128)(2,1)S(1)}, u32[]{:S(2)}, u32[]{:S(2)}) collective-permute-start(bf16[1,125,256]{2,1,0:T(8,128)(2,1)S(1)} %get-tuple-element.591), channel_id=1, source_target_pairs={{0,1},{1,2},{2,3},{3,4},{4,5},{5,6},{6,7},{8,9},{9,10},{10,11},{11... | collective-permute-start | bytes 192008 | tf_op jit(solution)/shard_map/while/body/eval_jaxpr/ppermute | solution.py:16
  55.8 6.2 %collective-permute-start = (bf16[1,125,256]{2,1,0:T(8,128)(2,1)S(1)}, bf16[1,125,256]{2,1,0:T(8,128)(2,1)S(1)}, u32[]{:S(2)}, u32[]{:S(2)}) collective-permute-start(bf16[1,125,256]{2,1,0:T(8,128)(2,1)S(1)} %get-tuple-element.590), channel_id=1, source_target_pairs={{0,8},{8,16},{16,24},{1,9},{9,17},{17,25},{2,10},{10,18},{18,26},{... | collective-permute-start | bytes 192008 | tf_op jit(solution)/shard_map/while/body/eval_jaxpr/ppermute | solution.py:16
  62.0 7.3 %collective-permute-start.1 = (bf16[1,125,256]{2,1,0:T(8,128)(2,1)S(1)}, bf16[1,125,256]{2,1,0:T(8,128)(2,1)S(1)}, u32[]{:S(2)}, u32[]{:S(2)}) collective-permute-start(bf16[1,125,256]{2,1,0:T(8,128)(2,1)S(1)} %get-tuple-element.591), channel_id=1, source_target_pairs={{0,1},{1,2},{2,3},{3,4},{4,5},{5,6},{6,7},{8,9},{9,10},{10,11},{11... | collective-permute-start | bytes 192008 | tf_op jit(solution)/shard_map/while/body/eval_jaxpr/ppermute | solution.py:16
  63.3 6.2 %collective-permute-start = (bf16[1,125,256]{2,1,0:T(8,128)(2,1)S(1)}, bf16[1,125,256]{2,1,0:T(8,128)(2,1)S(1)}, u32[]{:S(2)}, u32[]{:S(2)}) collective-permute-start(bf16[1,125,256]{2,1,0:T(8,128)(2,1)S(1)} %get-tuple-element.590), channel_id=1, source_target_pairs={{0,8},{8,16},{16,24},{1,9},{9,17},{17,25},{2,10},{10,18},{18,26},{... | collective-permute-start | bytes 192008 | tf_op jit(solution)/shard_map/while/body/eval_jaxpr/ppermute | solution.py:16
  69.5 7.3 %collective-permute-start.1 = (bf16[1,125,256]{2,1,0:T(8,128)(2,1)S(1)}, bf16[1,125,256]{2,1,0:T(8,128)(2,1)S(1)}, u32[]{:S(2)}, u32[]{:S(2)}) collective-permute-start(bf16[1,125,256]{2,1,0:T(8,128)(2,1)S(1)} %get-tuple-element.591), channel_id=1, source_target_pairs={{0,1},{1,2},{2,3},{3,4},{4,5},{5,6},{6,7},{8,9},{9,10},{10,11},{11... | collective-permute-start | bytes 192008 | tf_op jit(solution)/shard_map/while/body/eval_jaxpr/ppermute | solution.py:16
  70.8 6.2 %collective-permute-start = (bf16[1,125,256]{2,1,0:T(8,128)(2,1)S(1)}, bf16[1,125,256]{2,1,0:T(8,128)(2,1)S(1)}, u32[]{:S(2)}, u32[]{:S(2)}) collective-permute-start(bf16[1,125,256]{2,1,0:T(8,128)(2,1)S(1)} %get-tuple-element.590), channel_id=1, source_target_pairs={{0,8},{8,16},{16,24},{1,9},{9,17},{17,25},{2,10},{10,18},{18,26},{... | collective-permute-start | bytes 192008 | tf_op jit(solution)/shard_map/while/body/eval_jaxpr/ppermute | solution.py:16
  77.0 7.3 %collective-permute-start.1 = (bf16[1,125,256]{2,1,0:T(8,128)(2,1)S(1)}, bf16[1,125,256]{2,1,0:T(8,128)(2,1)S(1)}, u32[]{:S(2)}, u32[]{:S(2)}) collective-permute-start(bf16[1,125,256]{2,1,0:T(8,128)(2,1)S(1)} %get-tuple-element.591), channel_id=1, source_target_pairs={{0,1},{1,2},{2,3},{3,4},{4,5},{5,6},{6,7},{8,9},{9,10},{10,11},{11... | collective-permute-start | bytes 192008 | tf_op jit(solution)/shard_map/while/body/eval_jaxpr/ppermute | solution.py:16
  78.3 6.2 %collective-permute-start = (bf16[1,125,256]{2,1,0:T(8,128)(2,1)S(1)}, bf16[1,125,256]{2,1,0:T(8,128)(2,1)S(1)}, u32[]{:S(2)}, u32[]{:S(2)}) collective-permute-start(bf16[1,125,256]{2,1,0:T(8,128)(2,1)S(1)} %get-tuple-element.590), channel_id=1, source_target_pairs={{0,8},{8,16},{16,24},{1,9},{9,17},{17,25},{2,10},{10,18},{18,26},{... | collective-permute-start | bytes 192008 | tf_op jit(solution)/shard_map/while/body/eval_jaxpr/ppermute | solution.py:16
  84.5 64.8 %collective-permute-start.1 = (bf16[1,125,256]{2,1,0:T(8,128)(2,1)S(1)}, bf16[1,125,256]{2,1,0:T(8,128)(2,1)S(1)}, u32[]{:S(2)}, u32[]{:S(2)}) collective-permute-start(bf16[1,125,256]{2,1,0:T(8,128)(2,1)S(1)} %get-tuple-element.591), channel_id=1, source_target_pairs={{0,1},{1,2},{2,3},{3,4},{4,5},{5,6},{6,7},{8,9},{9,10},{10,11},{11... | collective-permute-start | bytes 192008 | tf_op jit(solution)/shard_map/while/body/eval_jaxpr/ppermute | solution.py:16
  85.8 63.7 %collective-permute-start = (bf16[1,125,256]{2,1,0:T(8,128)(2,1)S(1)}, bf16[1,125,256]{2,1,0:T(8,128)(2,1)S(1)}, u32[]{:S(2)}, u32[]{:S(2)}) collective-permute-start(bf16[1,125,256]{2,1,0:T(8,128)(2,1)S(1)} %get-tuple-element.590), channel_id=1, source_target_pairs={{0,8},{8,16},{16,24},{1,9},{9,17},{17,25},{2,10},{10,18},{18,26},{... | collective-permute-start | bytes 192008 | tf_op jit(solution)/shard_map/while/body/eval_jaxpr/ppermute | solution.py:16
  157.6 7.3 %collective-permute-start.1 = (bf16[1,125,256]{2,1,0:T(8,128)(2,1)S(1)}, bf16[1,125,256]{2,1,0:T(8,128)(2,1)S(1)}, u32[]{:S(2)}, u32[]{:S(2)}) collective-permute-start(bf16[1,125,256]{2,1,0:T(8,128)(2,1)S(1)} %get-tuple-element.591), channel_id=1, source_target_pairs={{0,1},{1,2},{2,3},{3,4},{4,5},{5,6},{6,7},{8,9},{9,10},{10,11},{11... | collective-permute-start | bytes 192008 | tf_op jit(solution)/shard_map/while/body/eval_jaxpr/ppermute | solution.py:16
  158.9 6.2 %collective-permute-start = (bf16[1,125,256]{2,1,0:T(8,128)(2,1)S(1)}, bf16[1,125,256]{2,1,0:T(8,128)(2,1)S(1)}, u32[]{:S(2)}, u32[]{:S(2)}) collective-permute-start(bf16[1,125,256]{2,1,0:T(8,128)(2,1)S(1)} %get-tuple-element.590), channel_id=1, source_target_pairs={{0,8},{8,16},{16,24},{1,9},{9,17},{17,25},{2,10},{10,18},{18,26},{... | collective-permute-start | bytes 192008 | tf_op jit(solution)/shard_map/while/body/eval_jaxpr/ppermute | solution.py:16
  173.2 7.3 %collective-permute-start.1 = (bf16[1,125,256]{2,1,0:T(8,128)(2,1)S(1)}, bf16[1,125,256]{2,1,0:T(8,128)(2,1)S(1)}, u32[]{:S(2)}, u32[]{:S(2)}) collective-permute-start(bf16[1,125,256]{2,1,0:T(8,128)(2,1)S(1)} %get-tuple-element.591), channel_id=1, source_target_pairs={{0,1},{1,2},{2,3},{3,4},{4,5},{5,6},{6,7},{8,9},{9,10},{10,11},{11... | collective-permute-start | bytes 192008 | tf_op jit(solution)/shard_map/while/body/eval_jaxpr/ppermute | solution.py:16
  174.5 6.2 %collective-permute-start = (bf16[1,125,256]{2,1,0:T(8,128)(2,1)S(1)}, bf16[1,125,256]{2,1,0:T(8,128)(2,1)S(1)}, u32[]{:S(2)}, u32[]{:S(2)}) collective-permute-start(bf16[1,125,256]{2,1,0:T(8,128)(2,1)S(1)} %get-tuple-element.590), channel_id=1, source_target_pairs={{0,8},{8,16},{16,24},{1,9},{9,17},{17,25},{2,10},{10,18},{18,26},{... | collective-permute-start | bytes 192008 | tf_op jit(solution)/shard_map/while/body/eval_jaxpr/ppermute | solution.py:16
  188.7 7.3 %collective-permute-start.1 = (bf16[1,125,256]{2,1,0:T(8,128)(2,1)S(1)}, bf16[1,125,256]{2,1,0:T(8,128)(2,1)S(1)}, u32[]{:S(2)}, u32[]{:S(2)}) collective-permute-start(bf16[1,125,256]{2,1,0:T(8,128)(2,1)S(1)} %get-tuple-element.591), channel_id=1, source_target_pairs={{0,1},{1,2},{2,3},{3,4},{4,5},{5,6},{6,7},{8,9},{9,10},{10,11},{11... | collective-permute-start | bytes 192008 | tf_op jit(solution)/shard_map/while/body/eval_jaxpr/ppermute | solution.py:16
  190.0 6.2 %collective-permute-start = (bf16[1,125,256]{2,1,0:T(8,128)(2,1)S(1)}, bf16[1,125,256]{2,1,0:T(8,128)(2,1)S(1)}, u32[]{:S(2)}, u32[]{:S(2)}) collective-permute-start(bf16[1,125,256]{2,1,0:T(8,128)(2,1)S(1)} %get-tuple-element.590), channel_id=1, source_target_pairs={{0,8},{8,16},{16,24},{1,9},{9,17},{17,25},{2,10},{10,18},{18,26},{... | collective-permute-start | bytes 192008 | tf_op jit(solution)/shard_map/while/body/eval_jaxpr/ppermute | solution.py:16
  204.3 7.3 %collective-permute-start.1 = (bf16[1,125,256]{2,1,0:T(8,128)(2,1)S(1)}, bf16[1,125,256]{2,1,0:T(8,128)(2,1)S(1)}, u32[]{:S(2)}, u32[]{:S(2)}) collective-permute-start(bf16[1,125,256]{2,1,0:T(8,128)(2,1)S(1)} %get-tuple-element.591), channel_id=1, source_target_pairs={{0,1},{1,2},{2,3},{3,4},{4,5},{5,6},{6,7},{8,9},{9,10},{10,11},{11... | collective-permute-start | bytes 192008 | tf_op jit(solution)/shard_map/while/body/eval_jaxpr/ppermute | solution.py:16
  205.6 6.2 %collective-permute-start = (bf16[1,125,256]{2,1,0:T(8,128)(2,1)S(1)}, bf16[1,125,256]{2,1,0:T(8,128)(2,1)S(1)}, u32[]{:S(2)}, u32[]{:S(2)}) collective-permute-start(bf16[1,125,256]{2,1,0:T(8,128)(2,1)S(1)} %get-tuple-element.590), channel_id=1, source_target_pairs={{0,8},{8,16},{16,24},{1,9},{9,17},{17,25},{2,10},{10,18},{18,26},{... | collective-permute-start | bytes 192008 | tf_op jit(solution)/shard_map/while/body/eval_jaxpr/ppermute | solution.py:16
  219.8 7.3 %collective-permute-start.1 = (bf16[1,125,256]{2,1,0:T(8,128)(2,1)S(1)}, bf16[1,125,256]{2,1,0:T(8,128)(2,1)S(1)}, u32[]{:S(2)}, u32[]{:S(2)}) collective-permute-start(bf16[1,125,256]{2,1,0:T(8,128)(2,1)S(1)} %get-tuple-element.591), channel_id=1, source_target_pairs={{0,1},{1,2},{2,3},{3,4},{4,5},{5,6},{6,7},{8,9},{9,10},{10,11},{11... | collective-permute-start | bytes 192008 | tf_op jit(solution)/shard_map/while/body/eval_jaxpr/ppermute | solution.py:16
  221.1 6.2 %collective-permute-start = (bf16[1,125,256]{2,1,0:T(8,128)(2,1)S(1)}, bf16[1,125,256]{2,1,0:T(8,128)(2,1)S(1)}, u32[]{:S(2)}, u32[]{:S(2)}) collective-permute-start(bf16[1,125,256]{2,1,0:T(8,128)(2,1)S(1)} %get-tuple-element.590), channel_id=1, source_target_pairs={{0,8},{8,16},{16,24},{1,9},{9,17},{17,25},{2,10},{10,18},{18,26},{... | collective-permute-start | bytes 192008 | tf_op jit(solution)/shard_map/while/body/eval_jaxpr/ppermute | solution.py:16
  235.4 7.3 %collective-permute-start.1 = (bf16[1,125,256]{2,1,0:T(8,128)(2,1)S(1)}, bf16[1,125,256]{2,1,0:T(8,128)(2,1)S(1)}, u32[]{:S(2)}, u32[]{:S(2)}) collective-permute-start(bf16[1,125,256]{2,1,0:T(8,128)(2,1)S(1)} %get-tuple-element.591), channel_id=1, source_target_pairs={{0,1},{1,2},{2,3},{3,4},{4,5},{5,6},{6,7},{8,9},{9,10},{10,11},{11... | collective-permute-start | bytes 192008 | tf_op jit(solution)/shard_map/while/body/eval_jaxpr/ppermute | solution.py:16
  236.7 6.2 %collective-permute-start = (bf16[1,125,256]{2,1,0:T(8,128)(2,1)S(1)}, bf16[1,125,256]{2,1,0:T(8,128)(2,1)S(1)}, u32[]{:S(2)}, u32[]{:S(2)}) collective-permute-start(bf16[1,125,256]{2,1,0:T(8,128)(2,1)S(1)} %get-tuple-element.590), channel_id=1, source_target_pairs={{0,8},{8,16},{16,24},{1,9},{9,17},{17,25},{2,10},{10,18},{18,26},{... | collective-permute-start | bytes 192008 | tf_op jit(solution)/shard_map/while/body/eval_jaxpr/ppermute | solution.py:16
  250.9 7.3 %collective-permute-start.1 = (bf16[1,125,256]{2,1,0:T(8,128)(2,1)S(1)}, bf16[1,125,256]{2,1,0:T(8,128)(2,1)S(1)}, u32[]{:S(2)}, u32[]{:S(2)}) collective-permute-start(bf16[1,125,256]{2,1,0:T(8,128)(2,1)S(1)} %get-tuple-element.591), channel_id=1, source_target_pairs={{0,1},{1,2},{2,3},{3,4},{4,5},{5,6},{6,7},{8,9},{9,10},{10,11},{11... | collective-permute-start | bytes 192008 | tf_op jit(solution)/shard_map/while/body/eval_jaxpr/ppermute | solution.py:16
  252.2 6.2 %collective-permute-start = (bf16[1,125,256]{2,1,0:T(8,128)(2,1)S(1)}, bf16[1,125,256]{2,1,0:T(8,128)(2,1)S(1)}, u32[]{:S(2)}, u32[]{:S(2)}) collective-permute-start(bf16[1,125,256]{2,1,0:T(8,128)(2,1)S(1)} %get-tuple-element.590), channel_id=1, source_target_pairs={{0,8},{8,16},{16,24},{1,9},{9,17},{17,25},{2,10},{10,18},{18,26},{... | collective-permute-start | bytes 192008 | tf_op jit(solution)/shard_map/while/body/eval_jaxpr/ppermute | solution.py:16
where the time goes:
time: 271 us; the launch traced here: 268 us
  waiting for transfers between devices  141 us (52%)
  starting transfers between devices  46.4 us (17%)
  local copies, waits for them, and re-layouts  26.7 us (10%)
  matrix products  20.3 us (7%)
  other arithmetic  17.2 us (6%)
  loops' own time  16.3 us (6%)
    ppermute x36, waiting for transfers between devices, from_behind(): return lax.ppermute(block, axis, route)  141 us
    ppermute x36, starting transfers between devices, from_behind(): return lax.ppermute(block, axis, route)  46.4 us
    dot_general x8, matrix products, solve_block(): jnp.dot(block, source, preferred_element_type=jnp.float32)  18.3 us
    another operation x18, loops' own time, step_now(): lax.cond(is_live, advance_now, hold_now, (x_in, y_in, x_out, y_out, z_tra...  15.5 us
    unnamed x4, local copies, waits for them, and re-layouts  13.5 us
    reduce_sum x8, other arithmetic, slot_of(): return jnp.sum(jnp.where(plane_ids == plane, order_row, 0))  10.4 us
    reduce_sum x8, other arithmetic, select_matrices(): jnp.sum(jnp.where(orients[..., None, None] == codes, lookup, 0), axis=-2)  6.19 us
    eq x8, local copies, waits for them, and re-layouts, select_matrices(): orients[..., None, None] == codes  5.53 us
  transfers between devices with their start and end apart: 36, of which 35 were waited for; matrix products, arithmetic and copies ran while one was open for 0% of the time, Pallas kernels for 0%

commit v1 on v0

v1 whole, which is shorter than its diff:
```python
import functools

import jax
import jax.numpy as jnp
import numpy as np
from jax import lax
from jax.experimental import pallas as pl
from jax.experimental.pallas import tpu as pltpu
from jax.sharding import PartitionSpec as P

VARS = 5
NODES = 5
SQUARE = NODES * NODES
FACE = VARS * SQUARE
BLOCK = FACE * NODES
LANE = 128
CHUNKS = 2
MESH = pl.DeviceIdType.MESH


def orient_table():
    table = np.zeros((8, LANE, LANE), np.float32)
    for orient in range(8):
        for variable in range(VARS):
            for first in range(NODES):
                for second in range(NODES):
                    p, q = (second, first) if orient & 1 else (first, second)
                    if orient & 2:
                        p = NODES - 1 - p
                    if orient & 4:
                        q = NODES - 1 - q
                    target = variable * SQUARE + first * NODES + second
                    table[orient, target, variable * SQUARE + p * NODES + q] = 1.0
    return table


def dot(a, b):
    return jnp.dot(a, b, preferred_element_type=jnp.float32)


def sweep_kernel(
    order, orient, table_hbm, lift_hbm, rhs_hbm, inv_hbm, sol,
    table, lift, rhs, inv, padded, turned, full_m, wide_m, part_m, full_r, trace_m, trace_r,
    inc, out, load_sem, x_send, y_send, x_recv, y_recv,
):
    planes, columns = rhs.shape[0], rhs.shape[2]
    width = columns // CHUNKS
    two, three = 2 * LANE, 3 * LANE
    count_x, count_y = lax.axis_size("gx"), lax.axis_size("gy")
    me_x, me_y = lax.axis_index("gx"), lax.axis_index("gy")
    has_left, has_right = me_x > 0, me_x < count_x - 1
    has_below, has_above = me_y > 0, me_y < count_y - 1

    loads = [
        pltpu.make_async_copy(source, target, load_sem.at[i])
        for i, (source, target) in enumerate(
            [(lift_hbm, lift), (table_hbm, table), (rhs_hbm, rhs), (inv_hbm, inv)]
        )
    ]
    for load in loads:
        load.start()

    barrier = pltpu.get_barrier_semaphore()
    for present, x, y in (
        (has_left, me_x - 1, me_y),
        (has_right, me_x + 1, me_y),
        (has_below, me_x, me_y - 1),
        (has_above, me_x, me_y + 1),
    ):
        @pl.when(present)
        def _():
            pl.semaphore_signal(barrier, inc=1, device_id=(x, y), device_id_type=MESH)

    part_m[...] = jnp.zeros_like(part_m)
    trace_r[...] = jnp.zeros_like(trace_r)
    out[0] = jnp.zeros(out.shape[1:], out.dtype)

    @pl.when(me_x == 0)
    def _():
        inc[:, :, :LANE, :] = jnp.zeros((planes, CHUNKS, LANE, width), inc.dtype)

    @pl.when(me_y == 0)
    def _():
        inc[:, :, LANE:, :] = jnp.zeros((planes, CHUNKS, LANE, width), inc.dtype)

    row = lax.broadcasted_iota(jnp.int32, (3 * FACE, three), 0)
    col = lax.broadcasted_iota(jnp.int32, (3 * FACE, three), 1)
    face = jnp.where(col >= two, 2, jnp.where(col >= LANE, 1, 0))
    inside = col - face * LANE
    spread = ((inside < FACE) & (row == face * FACE + inside)).astype(jnp.float32).astype(jnp.bfloat16)
    loads[0].wait()
    padded[...] = dot(lift[...], spread).astype(jnp.bfloat16)
    for load in loads[1:]:
        load.wait()

    def pick(source, put):
        for v in range(VARS):
            put(v * SQUARE, source[pl.ds(v * FACE + FACE - SQUARE, SQUARE), :])
        for v in range(VARS * NODES):
            put(LANE + v * NODES, source[pl.ds(v * SQUARE + SQUARE - NODES, NODES), :])
        put(two, source[pl.ds(NODES - 1, FACE, stride=NODES), :])

    def prepare(k):
        slot = order[k]
        for d in range(3):
            tile = slice(d * LANE, (d + 1) * LANE)
            turned[:, tile] = dot(padded[:, tile], table[orient[slot * 3 + d]]).astype(jnp.bfloat16)
        block = inv[slot]
        moved = dot(block, turned[...])
        full_m[k] = moved.astype(jnp.bfloat16)
        for j in range(3):
            wide_m[j] = moved[:, j * LANE : (j + 1) * LANE]
        plain = dot(block, rhs[slot])
        for j in range(columns // LANE):
            full_r[k, j] = plain[:, j * LANE : (j + 1) * LANE]
        for j in range(3):
            def put_m(start, rows):
                part_m[j, pl.ds(start, rows.shape[0]), :] = rows
            pick(wide_m.at[j], put_m)
            trace_m[k, :, j * LANE : (j + 1) * LANE] = part_m[j].astype(jnp.bfloat16)
        for j in range(columns // LANE):
            def put_r(start, rows):
                trace_r[k, j, pl.ds(start, rows.shape[0]), :] = rows
            pick(full_r.at[k, j], put_r)

    def base_of(ref, k, c):
        per = width // LANE
        return jnp.concatenate([ref[k, c * per + j] for j in range(per)], axis=-1)

    def hop(k, c, axis):
        rows = pl.ds(axis * LANE, LANE)
        send, recv = ((x_send, x_recv), (y_send, y_recv))[axis]
        return pltpu.make_async_remote_copy(
            src_ref=out.at[k + 1, c, rows, :],
            dst_ref=inc.at[k, c, rows, :],
            send_sem=send.at[k, c],
            recv_sem=recv.at[k, c],
            device_id=((me_x + 1, me_y), (me_x, me_y + 1))[axis],
            device_id_type=MESH,
        )

    def advance(k, c):
        started = base_of(trace_r, k, c) - dot(trace_m[k, :, two:], out[k, c, two:, :])

        @pl.when(has_left)
        def _():
            hop(k, c, 0).wait_recv()

        @pl.when(has_below)
        def _():
            hop(k, c, 1).wait_recv()

        arrived = inc[k, c]
        out[k + 1, c, :two, :] = (started[:two] - dot(trace_m[k, :two, :two], arrived)).astype(jnp.bfloat16)

        @pl.when(has_above)
        def _():
            hop(k, c, 1).start()

        @pl.when(has_right)
        def _():
            hop(k, c, 0).start()

        out[k + 1, c, two:, :] = (started[two:] - dot(trace_m[k, two:, :two], arrived)).astype(jnp.bfloat16)

    def finish(k, c):
        lifted = dot(full_m[k, :, :two], inc[k, c]) + dot(full_m[k, :, two:], out[k, c, two:, :])
        sol[k, :, c * width : (c + 1) * width] = (base_of(full_r, k, c) - lifted).astype(jnp.bfloat16)

    lead = jnp.minimum(1 + 2 * (me_x + me_y), planes)

    def ahead(k, carry):
        prepare(k)
        return carry

    lax.fori_loop(0, lead, ahead, 0)

    neighbours = sum(p.astype(jnp.int32) for p in (has_left, has_right, has_below, has_above))
    pl.semaphore_wait(barrier, neighbours)

    def step(k, carry):
        for c in range(CHUNKS):
            advance(k, c)

        @pl.when(k + lead < planes)
        def _():
            prepare(k + lead)

        for c in range(CHUNKS):
            finish(k, c)
        return carry

    lax.fori_loop(0, planes, step, 0)

    def drain(k, carry):
        for c in range(CHUNKS):
            @pl.when(has_right)
            def _():
                hop(k, c, 0).wait_send()

            @pl.when(has_above)
            def _():
                hop(k, c, 1).wait_send()
        return carry

    lax.fori_loop(0, planes, drain, 0)


def place_kernel(order, sol, out, sems):
    planes = sol.shape[0]
    copies = [pltpu.make_async_copy(sol.at[k], out.at[order[k]], sems.at[k]) for k in range(planes)]
    for copy in copies:
        copy.start()
    for copy in copies:
        copy.wait()


def on_device(right_side, inverse_blocks, lift_matrix, plane_order, face_orient):
    rhs, inv = right_side[0, 0], inverse_blocks[0, 0]
    order = plane_order[0, 0]
    orient = face_orient[0, 0].reshape(-1)
    planes, block, columns = rhs.shape
    tiles = columns // LANE
    width = columns // CHUNKS
    two, three = 2 * LANE, 3 * LANE
    bf16, f32 = jnp.bfloat16, jnp.float32
    table = jnp.asarray(orient_table(), bf16)
    smem = pl.BlockSpec(memory_space=pltpu.SMEM)
    vmem = pl.BlockSpec(memory_space=pltpu.VMEM)
    anywhere = pl.BlockSpec(memory_space=pl.ANY)
    sol = pl.pallas_call(
        sweep_kernel,
        out_shape=jax.ShapeDtypeStruct(rhs.shape, bf16),
        in_specs=[smem, smem] + [anywhere] * 4,
        out_specs=vmem,
        scratch_shapes=[
            pltpu.VMEM(table.shape, bf16),
            pltpu.VMEM(lift_matrix.shape, bf16),
            pltpu.VMEM(rhs.shape, bf16),
            pltpu.VMEM(inv.shape, bf16),
            pltpu.VMEM((block, three), bf16),
            pltpu.VMEM((block, three), bf16),
            pltpu.VMEM((planes, block, three), bf16),
            pltpu.VMEM((3, block, LANE), f32),
            pltpu.VMEM((3, three, LANE), f32),
            pltpu.VMEM((planes, tiles, block, LANE), f32),
            pltpu.VMEM((planes, three, three), bf16),
            pltpu.VMEM((planes, tiles, three, LANE), f32),
            pltpu.VMEM((planes, CHUNKS, two, width), bf16),
            pltpu.VMEM((planes + 1, CHUNKS, three, width), bf16),
            pltpu.SemaphoreType.DMA((4,)),
            pltpu.SemaphoreType.DMA((planes, CHUNKS)),
            pltpu.SemaphoreType.DMA((planes, CHUNKS)),
            pltpu.SemaphoreType.DMA((planes, CHUNKS)),
            pltpu.SemaphoreType.DMA((planes, CHUNKS)),
        ],
        compiler_params=pltpu.CompilerParams(
            collective_id=0, has_side_effects=True, vmem_limit_bytes=56 * 1024 * 1024
        ),
    )(order, orient, table, lift_matrix, rhs, inv)
    result = pl.pallas_call(
        place_kernel,
        out_shape=jax.ShapeDtypeStruct(rhs.shape, bf16),
        in_specs=[smem, vmem],
        out_specs=anywhere,
        scratch_shapes=[pltpu.SemaphoreType.DMA((planes,))],
    )(order, sol)
    return result[None, None]


def solution(mesh):
    placed = (
        P("gx", "gy", None, None, None),
        P("gx", "gy", None, None, None),
        P(),
        P("gx", "gy", None),
        P("gx", "gy", None, None),
    )
    return jax.shard_map(
        on_device,
        mesh=mesh,
        in_specs=placed,
        out_specs=P("gx", "gy", None, None, None),
        check_vma=False,
    )
```

time: 271 us -> 74 us (0.27)
  waiting for transfers between devices: 141 us -> 0 us
  Pallas kernels: 0 us -> 56.5 us
  starting transfers between devices: 46.4 us -> 0 us
  matrix products: 20.3 us -> 0 us
  other arithmetic: 17.2 us -> 0 us
  loops' own time: 16.3 us -> 0 us
  local copies, waits for them, and re-layouts: 26.7 us -> 17.2 us
    ppermute x36 -> x0, waiting for transfers between devices: 141 us -> none  [from_behind(): return lax.ppermute(block, axis, route)]
    pallas_call x0 -> x2, Pallas kernels: none -> 56.5 us  [the longest x1 53.2 us: on_device(): pl.pallas_call(sweep_kernel, out_shape=jax.ShapeDtypeStruct(rhs.shape, bf...]
    ppermute x36 -> x0, starting transfers between devices: 46.4 us -> none  [from_behind(): return lax.ppermute(block, axis, route)]
    dot_general x16 -> x0, matrix products: 20.3 us -> none  [the longest x8 18.3 us: solve_block(): jnp.dot(block, source, preferred_element_type=jnp.float32)]
    reduce_sum x16 -> x0, other arithmetic: 16.6 us -> none  [the longest x8 10.4 us: slot_of(): return jnp.sum(jnp.where(plane_ids == plane, order_row, 0))]
    another operation x19 -> x0, loops' own time: 16.3 us -> none  [the longest x18 15.5 us: step_now(): lax.cond(is_live, advance_now, hold_now, (x_in, y_in, x_out, y_out, z_tra...]
    eq x8 -> x0, local copies, waits for them, and re-layouts: 5.53 us -> none  [select_matrices(): orients[..., None, None] == codes]
    broadcast_in_dim x4 -> x1, local copies, waits for them, and re-layouts: 0.2 us -> 3.73 us  [on_device(): return result[None, None]]
  transfers between devices with their start and end apart: 36 -> 0, of which waited for: 35 -> 0; matrix products, arithmetic and copies ran while one was open for 0% -> 0% of each run, Pallas kernels for 0% -> 0%
where the time goes in v1:
time: 74 us; the launch traced here: 73.7 us
  Pallas kernels  56.5 us (76%)
  local copies, waits for them, and re-layouts  17.2 us (23%)
    pallas_call x1, Pallas kernels, on_device(): pl.pallas_call(sweep_kernel, out_shape=jax.ShapeDtypeStruct(rhs.shape, bf...  53.2 us
    unnamed x4, local copies, waits for them, and re-layouts  12.9 us
    broadcast_in_dim x1, local copies, waits for them, and re-layouts, on_device(): return result[None, None]  3.73 us
    pallas_call x1, Pallas kernels, on_device(): pl.pallas_call(place_kernel, out_shape=jax.ShapeDtypeStruct(rhs.shape, bf...  3.29 us

profile of v1, /device:TPU:31, one launch (start us, length us, event | category | flops | bytes accessed | tf_op | source)
XLA Modules:
  0.0 73.7 jit_solution(14587376853988401402)
XLA Ops:
  0.0 0.8 %copy.12 = s32[1,1,8,3]{3,2,1,0:T(8,128)S(1)} copy(s32[1,1,8,3]{2,1,3,0:T(1,128)} %param.10) | data formatting | bytes 192 | tf_op args[4]
  0.8 0.6 reshape_squeeze.3.orient
  1.4 2.0 %copy.15.lift_hbm = bf16[625,375]{1,0:T(8,128)(2,1)} copy(bf16[625,375]{0,1:T(8,128)(2,1)} %param.8) | data formatting | bytes 937500 | tf_op args[2]
  3.4 3.8 %copy.20 = bf16[1,1,8,625,256]{4,3,2,1,0:T(8,128)(2,1)} copy(bf16[1,1,8,625,256]{4,2,3,1,0:T(8,128)(2,1)} %param.6) | data formatting | bytes 5120000 | tf_op args[0]
  7.1 6.4 %copy.19 = bf16[1,1,8,625,625]{4,3,2,1,0:T(8,128)(2,1)} copy(bf16[1,1,8,625,625]{4,2,3,1,0:T(8,128)(2,1)} %param.7) | data formatting | bytes 12500000 | tf_op args[1]
  13.5 53.2 %shard_map.64.sol = bf16[8,625,256]{2,1,0:T(8,128)(2,1)} custom-call(s32[8]{0:T(128)} %bitcast.13, s32[24]{0:T(128)} %reshape_squeeze.3.orient, bf16[8,128,128]{2,1,0:T(8,128)(2,1)} %constant.2.clone.table_hbm, bf16[625,375]{1,0:T(8,128)(2,1)} %copy.15.lift_hbm, bf16[8,625,256]{2,1,0:T(8,128)(2,1)} %bitcast.12, bf16[8,625,625]{2,1,0:T(8,128)(2,1)} %bitcast.10), custom_call_target="tpu_custom_call" | custom-call | tf_op jit(solution)/shard_map/pallas_call | solution.py:231
  66.7 3.3 %shard_map.65 = bf16[8,625,256]{2,1,0:T(8,128)(2,1)} custom-call(s32[8]{0:T(128)} %bitcast.14, bf16[8,625,256]{2,1,0:T(8,128)(2,1)} %shard_map.64.sol), custom_call_target="tpu_custom_call" | custom-call | tf_op jit(solution)/shard_map/pallas_call | solution.py:261
  70.0 3.7 %copy.16 = bf16[1,1,8,625,256]{4,2,3,1,0:T(8,128)(2,1)} copy(bf16[1,1,8,625,256]{4,3,2,1,0:T(8,128)(2,1)} %bitcast.11) | data formatting | bytes 5120000 | tf_op jit(solution)/shard_map/broadcast_in_dim | solution.py:268

commit v2 on v1

--- a/solution.py
+++ b/solution.py
@@ -38,14 +38,20 @@
     return jnp.dot(a, b, preferred_element_type=jnp.float32)
 
 
+def row_chunks(block):
+    return [(start, min(LANE, block - start)) for start in range(0, block, LANE)]
+
+
 def sweep_kernel(
     order, orient, table_hbm, lift_hbm, rhs_hbm, inv_hbm, sol,
-    table, lift, rhs, inv, padded, turned, full_m, wide_m, part_m, full_r, trace_m, trace_r,
-    inc, out, load_sem, x_send, y_send, x_recv, y_recv,
+    table, lift, raw_r, raw_b, stage, rhs, inv, padded, turned, wide, part, picked, trace_m, trace_r,
+    inc, out, load_sem, r_sem, b_sem, x_send, y_send, x_recv, y_recv,
 ):
-    planes, columns = rhs.shape[0], rhs.shape[2]
+    planes, block, columns = rhs.shape
     width = columns // CHUNKS
     two, three = 2 * LANE, 3 * LANE
+    chunks = row_chunks(block)
+    tiles = [(t, min(LANE, block - t)) for t in range(0, block, LANE)]
     count_x, count_y = lax.axis_size("gx"), lax.axis_size("gy")
     me_x, me_y = lax.axis_index("gx"), lax.axis_index("gy")
     has_left, has_right = me_x > 0, me_x < count_x - 1
@@ -53,12 +59,21 @@
 
     loads = [
         pltpu.make_async_copy(source, target, load_sem.at[i])
-        for i, (source, target) in enumerate(
-            [(lift_hbm, lift), (table_hbm, table), (rhs_hbm, rhs), (inv_hbm, inv)]
-        )
+        for i, (source, target) in enumerate([(lift_hbm, lift), (table_hbm, table)])
     ]
     for load in loads:
         load.start()
+
+    def fetch(i, start, size):
+        rows = pl.ds(start, size)
+        return (
+            pltpu.make_async_copy(rhs_hbm.at[rows], raw_r.at[rows], r_sem.at[i]),
+            pltpu.make_async_copy(inv_hbm.at[rows], raw_b.at[rows], b_sem.at[i]),
+        )
+
+    for i, (start, size) in enumerate(chunks):
+        for copy in fetch(i, start, size):
+            copy.start()
 
     barrier = pltpu.get_barrier_semaphore()
     for present, x, y in (
@@ -71,8 +86,7 @@
         def _():
             pl.semaphore_signal(barrier, inc=1, device_id=(x, y), device_id_type=MESH)
 
-    part_m[...] = jnp.zeros_like(part_m)
-    trace_r[...] = jnp.zeros_like(trace_r)
+    part[...] = jnp.zeros_like(part)
     out[0] = jnp.zeros(out.shape[1:], out.dtype)
 
     @pl.when(me_x == 0)
@@ -89,9 +103,36 @@
     inside = col - face * LANE
     spread = ((inside < FACE) & (row == face * FACE + inside)).astype(jnp.float32).astype(jnp.bfloat16)
     loads[0].wait()
-    padded[...] = dot(lift[...], spread).astype(jnp.bfloat16)
-    for load in loads[1:]:
-        load.wait()
+    padded[...] = lax.dot_general(
+        lift[...], spread, (((0,), (0,)), ((), ())), preferred_element_type=jnp.float32
+    ).astype(jnp.bfloat16)
+    loads[1].wait()
+
+    def split(raw, into, rows, size, lanes, t):
+        mixed = raw[rows, :, lanes].astype(jnp.float32)
+        wide_lanes = mixed.shape[-1]
+        stage[t, : size * planes, :wide_lanes] = mixed.reshape(size * planes, wide_lanes)
+        for s in range(planes):
+            apart = stage[t, pl.ds(s, size, stride=planes), :]
+            into[s, rows, lanes] = apart[:, :wide_lanes].astype(jnp.bfloat16)
+
+    def arrange(i, start, size):
+        for copy in fetch(i, start, size):
+            copy.wait()
+        rows = pl.ds(start, size)
+        for t, (first, wide_lanes) in enumerate(tiles):
+            split(raw_b, inv, rows, size, slice(first, first + wide_lanes), t)
+        for t in range(columns // LANE):
+            split(raw_r, rhs, rows, size, slice(t * LANE, (t + 1) * LANE), len(tiles) + t)
+
+    def arrange_full(i, carry):
+        arrange(i, pl.multiple_of(i * LANE, LANE), LANE)
+        return carry
+
+    whole = block // LANE
+    lax.fori_loop(0, whole, arrange_full, 0)
+    for i, (start, size) in list(enumerate(chunks))[whole:]:
+        arrange(i, start, size)
 
     def pick(source, put):
         for v in range(VARS):
@@ -104,28 +145,19 @@
         slot = order[k]
         for d in range(3):
             tile = slice(d * LANE, (d + 1) * LANE)
-            turned[:, tile] = dot(padded[:, tile], table[orient[slot * 3 + d]]).astype(jnp.bfloat16)
-        block = inv[slot]
-        moved = dot(block, turned[...])
-        full_m[k] = moved.astype(jnp.bfloat16)
-        for j in range(3):
-            wide_m[j] = moved[:, j * LANE : (j + 1) * LANE]
-        plain = dot(block, rhs[slot])
-        for j in range(columns // LANE):
-            full_r[k, j] = plain[:, j * LANE : (j + 1) * LANE]
-        for j in range(3):
-            def put_m(start, rows):
-                part_m[j, pl.ds(start, rows.shape[0]), :] = rows
-            pick(wide_m.at[j], put_m)
-            trace_m[k, :, j * LANE : (j + 1) * LANE] = part_m[j].astype(jnp.bfloat16)
-        for j in range(columns // LANE):
-            def put_r(start, rows):
-                trace_r[k, j, pl.ds(start, rows.shape[0]), :] = rows
-            pick(full_r.at[k, j], put_r)
-
-    def base_of(ref, k, c):
-        per = width // LANE
-        return jnp.concatenate([ref[k, c * per + j] for j in range(per)], axis=-1)
+            turned[k, :, tile] = dot(padded[:, tile], table[orient[d, 0, slot]]).astype(jnp.bfloat16)
+        for t, (first, wide_lanes) in enumerate(tiles):
+            wide[t, :, :wide_lanes] = inv[slot, :, first : first + wide_lanes].astype(jnp.float32)
+
+            def put(start, rows):
+                part[t, pl.ds(start, rows.shape[0]), :] = rows
+
+            pick(wide.at[t], put)
+            picked[:, first : first + wide_lanes] = part[t, :, :wide_lanes].astype(jnp.bfloat16)
+        trace_m[k] = dot(picked[...], turned[k]).astype(jnp.bfloat16)
+        plain = dot(picked[...], rhs[slot])
+        for c in range(CHUNKS):
+            trace_r[k, c] = plain[:, c * width : (c + 1) * width]
 
     def hop(k, c, axis):
         rows = pl.ds(axis * LANE, LANE)
@@ -140,7 +172,7 @@
         )
 
     def advance(k, c):
-        started = base_of(trace_r, k, c) - dot(trace_m[k, :, two:], out[k, c, two:, :])
+        started = trace_r[k, c] - dot(trace_m[k, :, two:], out[k, c, two:, :])
 
         @pl.when(has_left)
         def _():
@@ -163,11 +195,17 @@
 
         out[k + 1, c, two:, :] = (started[two:] - dot(trace_m[k, two:, :two], arrived)).astype(jnp.bfloat16)
 
-    def finish(k, c):
-        lifted = dot(full_m[k, :, :two], inc[k, c]) + dot(full_m[k, :, two:], out[k, c, two:, :])
-        sol[k, :, c * width : (c + 1) * width] = (base_of(full_r, k, c) - lifted).astype(jnp.bfloat16)
-
-    lead = jnp.minimum(1 + 2 * (me_x + me_y), planes)
+    def finish(k):
+        slot = order[k]
+        behind = jnp.concatenate([inc[k, c] for c in range(CHUNKS)], axis=-1)
+        under = jnp.concatenate([out[k, c, two:, :] for c in range(CHUNKS)], axis=-1)
+        lifted = dot(turned[k, :, :two], behind) + dot(turned[k, :, two:], under)
+        source = (rhs[slot].astype(jnp.float32) - lifted).astype(jnp.bfloat16)
+        sol[k] = dot(inv[slot], source).astype(jnp.bfloat16)
+
+    distance = me_x + me_y
+    lead = jnp.minimum(1 + 2 * distance, planes)
+    near = distance * 2 <= count_x + count_y - 2
 
     def ahead(k, carry):
         prepare(k)
@@ -186,11 +224,21 @@
         def _():
             prepare(k + lead)
 
-        for c in range(CHUNKS):
-            finish(k, c)
+        @pl.when(jnp.logical_not(near))
+        def _():
+            finish(k)
+
         return carry
 
     lax.fori_loop(0, planes, step, 0)
+
+    @pl.when(near)
+    def _():
+        def late(k, carry):
+            finish(k)
+            return carry
+
+        lax.fori_loop(0, planes, late, 0)
 
     def drain(k, carry):
         for c in range(CHUNKS):
@@ -206,66 +254,77 @@
     lax.fori_loop(0, planes, drain, 0)
 
 
-def place_kernel(order, sol, out, sems):
-    planes = sol.shape[0]
-    copies = [pltpu.make_async_copy(sol.at[k], out.at[order[k]], sems.at[k]) for k in range(planes)]
-    for copy in copies:
-        copy.start()
-    for copy in copies:
-        copy.wait()
+def place_kernel(order, sol, out, stage):
+    planes, rows, columns = sol.shape
+    for t in range(columns // LANE):
+        lanes = slice(t * LANE, (t + 1) * LANE)
+        for k in range(planes):
+            stage[t, pl.ds(order[k], rows, stride=planes), :] = sol[k, :, lanes].astype(jnp.float32)
+        out[:, :, lanes] = stage[t].reshape(rows, planes, LANE).astype(jnp.bfloat16)
 
 
 def on_device(right_side, inverse_blocks, lift_matrix, plane_order, face_orient):
-    rhs, inv = right_side[0, 0], inverse_blocks[0, 0]
+    rhs = jnp.transpose(right_side, (0, 1, 3, 2, 4))[0, 0]
+    inv = jnp.transpose(inverse_blocks, (0, 1, 3, 2, 4))[0, 0]
     order = plane_order[0, 0]
-    orient = face_orient[0, 0].reshape(-1)
-    planes, block, columns = rhs.shape
-    tiles = columns // LANE
+    orient = jnp.transpose(face_orient, (0, 3, 1, 2))[0]
+    block, planes, columns = rhs.shape
+    tiles = pl.cdiv(block, LANE)
+    chunks = len(row_chunks(block))
     width = columns // CHUNKS
     two, three = 2 * LANE, 3 * LANE
     bf16, f32 = jnp.bfloat16, jnp.float32
     table = jnp.asarray(orient_table(), bf16)
+    lift = lift_matrix.T
     smem = pl.BlockSpec(memory_space=pltpu.SMEM)
     vmem = pl.BlockSpec(memory_space=pltpu.VMEM)
     anywhere = pl.BlockSpec(memory_space=pl.ANY)
     sol = pl.pallas_call(
         sweep_kernel,
-        out_shape=jax.ShapeDtypeStruct(rhs.shape, bf16),
+        out_shape=jax.ShapeDtypeStruct((planes, block, columns), bf16),
         in_specs=[smem, smem] + [anywhere] * 4,
         out_specs=vmem,
         scratch_shapes=[
             pltpu.VMEM(table.shape, bf16),
-            pltpu.VMEM(lift_matrix.shape, bf16),
+            pltpu.VMEM(lift.shape, bf16),
             pltpu.VMEM(rhs.shape, bf16),
             pltpu.VMEM(inv.shape, bf16),
-            pltpu.VMEM((block, three), bf16),
+            pltpu.VMEM((tiles + columns // LANE, LANE * planes, LANE), f32),
+            pltpu.VMEM((planes, block, columns), bf16),
+            pltpu.VMEM((planes, block, block), bf16),
             pltpu.VMEM((block, three), bf16),
             pltpu.VMEM((planes, block, three), bf16),
-            pltpu.VMEM((3, block, LANE), f32),
-            pltpu.VMEM((3, three, LANE), f32),
-            pltpu.VMEM((planes, tiles, block, LANE), f32),
+            pltpu.VMEM((tiles, block, LANE), f32),
+            pltpu.VMEM((tiles, three, LANE), f32),
+            pltpu.VMEM((three, block), bf16),
             pltpu.VMEM((planes, three, three), bf16),
-            pltpu.VMEM((planes, tiles, three, LANE), f32),
+            pltpu.VMEM((planes, CHUNKS, three, width), f32),
             pltpu.VMEM((planes, CHUNKS, two, width), bf16),
             pltpu.VMEM((planes + 1, CHUNKS, three, width), bf16),
-            pltpu.SemaphoreType.DMA((4,)),
+            pltpu.SemaphoreType.DMA((2,)),
+            pltpu.SemaphoreType.DMA((chunks,)),
+            pltpu.SemaphoreType.DMA((chunks,)),
             pltpu.SemaphoreType.DMA((planes, CHUNKS)),
             pltpu.SemaphoreType.DMA((planes, CHUNKS)),
             pltpu.SemaphoreType.DMA((planes, CHUNKS)),
             pltpu.SemaphoreType.DMA((planes, CHUNKS)),
         ],
         compiler_params=pltpu.CompilerParams(
-            collective_id=0, has_side_effects=True, vmem_limit_bytes=56 * 1024 * 1024
+            collective_id=0, has_side_effects=True, vmem_limit_bytes=60 * 1024 * 1024
         ),
-    )(order, orient, table, lift_matrix, rhs, inv)
+    )(order, orient, table, lift, rhs, inv)
     result = pl.pallas_call(
         place_kernel,
         out_shape=jax.ShapeDtypeStruct(rhs.shape, bf16),
-        in_specs=[smem, vmem],
-        out_specs=anywhere,
-        scratch_shapes=[pltpu.SemaphoreType.DMA((planes,))],
+        grid_spec=pltpu.PrefetchScalarGridSpec(
+            num_scalar_prefetch=1,
+            grid=(chunks,),
+            in_specs=[pl.BlockSpec((planes, LANE, columns), lambda i, o: (0, i, 0))],
+            out_specs=pl.BlockSpec((LANE, planes, columns), lambda i, o: (i, 0, 0)),
+            scratch_shapes=[pltpu.VMEM((columns // LANE, LANE * planes, LANE), f32)],
+        ),
     )(order, sol)
-    return result[None, None]
+    return jnp.transpose(result[None, None], (0, 1, 3, 2, 4))
 
 
 def solution(mesh):

time: 74 us -> 61.3 us (0.83)
  local copies, waits for them, and re-layouts: 17.2 us -> 0 us
  Pallas kernels: 56.5 us -> 61.1 us
    unnamed x4 -> x0, local copies, waits for them, and re-layouts: 12.9 us -> none
    broadcast_in_dim x1 -> x0, local copies, waits for them, and re-layouts: 3.73 us -> none  [on_device(): return result[None, None]]
    pallas_call x1, Pallas kernels: 3.29 us -> 6.02 us  [on_device(): pl.pallas_call(place_kernel, out_shape=jax.ShapeDtypeStruct(rhs.shape, bf...]
    pallas_call x1, Pallas kernels: 53.2 us -> 55.1 us  [on_device(): pl.pallas_call(sweep_kernel, out_shape=jax.ShapeDtypeStruct((planes, bloc...]
where the time goes in v2:
time: 61.3 us; the launch traced here: 61.1 us
  Pallas kernels  61.1 us (100%)
    pallas_call x1, Pallas kernels, on_device(): pl.pallas_call(sweep_kernel, out_shape=jax.ShapeDtypeStruct((planes, bloc...  55.1 us
    pallas_call x1, Pallas kernels, on_device(): pl.pallas_call(place_kernel, out_shape=jax.ShapeDtypeStruct(rhs.shape, bf...  6.02 us

profile of v2, /device:TPU:31, one launch (start us, length us, event | category | flops | bytes accessed | tf_op | source)
XLA Modules:
  0.0 61.1 jit_solution(16785377009368546460)
XLA Ops:
  0.0 55.1 %shard_map.64.sol = bf16[8,625,256]{2,1,0:T(8,128)(2,1)} custom-call(s32[8]{0:T(128)} %bitcast.17, s32[3,1,8]{2,1,0:T(1,128)} %bitcast.19, bf16[8,128,128]{2,1,0:T(8,128)(2,1)} %constant.2.clone.table_hbm, bf16[375,625]{1,0:T(8,128)(2,1)} %bitcast.16, bf16[625,8,256]{2,1,0:T(8,128)(2,1)} %bitcast.15, bf16[625,8,625]{2,1,0:T(8,128)(2,1)} %bitcast.14), custom_call_target="tpu_custom_call" | custom-call | tf_op jit(solution)/shard_map/pallas_call | solution.py:282
  55.1 6.0 %shard_map.65 = bf16[625,8,256]{2,1,0:T(8,128)(2,1)} custom-call(s32[8]{0:T(128)} %bitcast.18, bf16[8,625,256]{2,1,0:T(8,128)(2,1)} %shard_map.64.sol), custom_call_target="tpu_custom_call" | custom-call | tf_op jit(solution)/shard_map/pallas_call | solution.py:316

commit v3 on v2

--- a/solution.py
+++ b/solution.py
@@ -71,7 +71,9 @@
             pltpu.make_async_copy(inv_hbm.at[rows], raw_b.at[rows], b_sem.at[i]),
         )
 
-    for i, (start, size) in enumerate(chunks):
+    whole = block // LANE
+    depth = min(2, len(chunks))
+    for i, (start, size) in list(enumerate(chunks))[:depth]:
         for copy in fetch(i, start, size):
             copy.start()
 
@@ -119,6 +121,18 @@
     def arrange(i, start, size):
         for copy in fetch(i, start, size):
             copy.wait()
+        if size == LANE:
+            @pl.when(i + depth < whole)
+            def _():
+                for copy in fetch(i + depth, pl.multiple_of(start + depth * LANE, LANE), LANE):
+                    copy.start()
+
+            if whole < len(chunks):
+                @pl.when(i + depth == whole)
+                def _():
+                    for copy in fetch(whole, *chunks[whole]):
+                        copy.start()
+
         rows = pl.ds(start, size)
         for t, (first, wide_lanes) in enumerate(tiles):
             split(raw_b, inv, rows, size, slice(first, first + wide_lanes), t)
@@ -129,7 +143,6 @@
         arrange(i, pl.multiple_of(i * LANE, LANE), LANE)
         return carry
 
-    whole = block // LANE
     lax.fori_loop(0, whole, arrange_full, 0)
     for i, (start, size) in list(enumerate(chunks))[whole:]:
         arrange(i, start, size)
@@ -143,18 +156,18 @@
 
     def prepare(k):
         slot = order[k]
+        for t, (first, wide_lanes) in enumerate(tiles):
+            wide[t, :, :wide_lanes] = inv[slot, :, first : first + wide_lanes].astype(jnp.float32)
+
+            def put(start, rows):
+                part[t, pl.ds(start, rows.shape[0]), :] = rows
+
+            pick(wide.at[t], put)
+            picked[:, first : first + wide_lanes] = part[t, :, :wide_lanes].astype(jnp.bfloat16)
+        moved = dot(picked[...], padded[...]).astype(jnp.bfloat16)
         for d in range(3):
             tile = slice(d * LANE, (d + 1) * LANE)
-            turned[k, :, tile] = dot(padded[:, tile], table[orient[d, 0, slot]]).astype(jnp.bfloat16)
-        for t, (first, wide_lanes) in enumerate(tiles):
-            wide[t, :, :wide_lanes] = inv[slot, :, first : first + wide_lanes].astype(jnp.float32)
-
-            def put(start, rows):
-                part[t, pl.ds(start, rows.shape[0]), :] = rows
-
-            pick(wide.at[t], put)
-            picked[:, first : first + wide_lanes] = part[t, :, :wide_lanes].astype(jnp.bfloat16)
-        trace_m[k] = dot(picked[...], turned[k]).astype(jnp.bfloat16)
+            trace_m[k, :, tile] = dot(moved[:, tile], table[orient[d, 0, slot]]).astype(jnp.bfloat16)
         plain = dot(picked[...], rhs[slot])
         for c in range(CHUNKS):
             trace_r[k, c] = plain[:, c * width : (c + 1) * width]
@@ -183,11 +196,14 @@
             hop(k, c, 1).wait_recv()
 
         arrived = inc[k, c]
-        out[k + 1, c, :two, :] = (started[:two] - dot(trace_m[k, :two, :two], arrived)).astype(jnp.bfloat16)
+        ahead_rows = (started[:two] - dot(trace_m[k, :two, :two], arrived)).astype(jnp.bfloat16)
+        out[k + 1, c, LANE:two, :] = ahead_rows[LANE:]
 
         @pl.when(has_above)
         def _():
             hop(k, c, 1).start()
+
+        out[k + 1, c, :LANE, :] = ahead_rows[:LANE]
 
         @pl.when(has_right)
         def _():
@@ -197,9 +213,12 @@
 
     def finish(k):
         slot = order[k]
-        behind = jnp.concatenate([inc[k, c] for c in range(CHUNKS)], axis=-1)
-        under = jnp.concatenate([out[k, c, two:, :] for c in range(CHUNKS)], axis=-1)
-        lifted = dot(turned[k, :, :two], behind) + dot(turned[k, :, two:], under)
+        faces = [[inc[k, c, d * LANE : (d + 1) * LANE, :] for c in range(CHUNKS)] for d in range(2)]
+        faces.append([out[k, c, two:, :] for c in range(CHUNKS)])
+        for d in range(3):
+            face = jnp.concatenate(faces[d], axis=-1)
+            turned[d * LANE : (d + 1) * LANE, :] = dot(table[orient[d, 0, slot]], face).astype(jnp.bfloat16)
+        lifted = dot(padded[...], turned[...])
         source = (rhs[slot].astype(jnp.float32) - lifted).astype(jnp.bfloat16)
         sol[k] = dot(inv[slot], source).astype(jnp.bfloat16)
 
@@ -254,13 +273,35 @@
     lax.fori_loop(0, planes, drain, 0)
 
 
-def place_kernel(order, sol, out, stage):
-    planes, rows, columns = sol.shape
-    for t in range(columns // LANE):
-        lanes = slice(t * LANE, (t + 1) * LANE)
-        for k in range(planes):
-            stage[t, pl.ds(order[k], rows, stride=planes), :] = sol[k, :, lanes].astype(jnp.float32)
-        out[:, :, lanes] = stage[t].reshape(rows, planes, LANE).astype(jnp.bfloat16)
+def place_kernel(order, sol, out, stage, ready, sems):
+    planes, block, columns = sol.shape
+    chunks = row_chunks(block)
+    whole = block // LANE
+
+    def put(i, start, size):
+        rows = pl.ds(start, size)
+        return pltpu.make_async_copy(ready.at[rows], out.at[rows], sems.at[i])
+
+    def place(i, start, size):
+        rows = pl.ds(start, size)
+        for t in range(columns // LANE):
+            lanes = slice(t * LANE, (t + 1) * LANE)
+            for k in range(planes):
+                stage[t, pl.ds(order[k], size, stride=planes), :] = sol[k, rows, lanes].astype(jnp.float32)
+            ready[rows, :, lanes] = (
+                stage[t, : size * planes, :].reshape(size, planes, LANE).astype(jnp.bfloat16)
+            )
+        put(i, start, size).start()
+
+    def place_full(i, carry):
+        place(i, pl.multiple_of(i * LANE, LANE), LANE)
+        return carry
+
+    lax.fori_loop(0, whole, place_full, 0)
+    for i, (start, size) in list(enumerate(chunks))[whole:]:
+        place(i, start, size)
+    for i, (start, size) in enumerate(chunks):
+        put(i, start, size).wait()
 
 
 def on_device(right_side, inverse_blocks, lift_matrix, plane_order, face_orient):
@@ -281,7 +322,7 @@
     anywhere = pl.BlockSpec(memory_space=pl.ANY)
     sol = pl.pallas_call(
         sweep_kernel,
-        out_shape=jax.ShapeDtypeStruct((planes, block, columns), bf16),
+        out_shape=pltpu.VMEM((planes, block, columns), bf16),
         in_specs=[smem, smem] + [anywhere] * 4,
         out_specs=vmem,
         scratch_shapes=[
@@ -293,7 +334,7 @@
             pltpu.VMEM((planes, block, columns), bf16),
             pltpu.VMEM((planes, block, block), bf16),
             pltpu.VMEM((block, three), bf16),
-            pltpu.VMEM((planes, block, three), bf16),
+            pltpu.VMEM((three, columns), bf16),
             pltpu.VMEM((tiles, block, LANE), f32),
             pltpu.VMEM((tiles, three, LANE), f32),
             pltpu.VMEM((three, block), bf16),
@@ -316,13 +357,14 @@
     result = pl.pallas_call(
         place_kernel,
         out_shape=jax.ShapeDtypeStruct(rhs.shape, bf16),
-        grid_spec=pltpu.PrefetchScalarGridSpec(
-            num_scalar_prefetch=1,
-            grid=(chunks,),
-            in_specs=[pl.BlockSpec((planes, LANE, columns), lambda i, o: (0, i, 0))],
-            out_specs=pl.BlockSpec((LANE, planes, columns), lambda i, o: (i, 0, 0)),
-            scratch_shapes=[pltpu.VMEM((columns // LANE, LANE * planes, LANE), f32)],
-        ),
+        in_specs=[smem, vmem],
+        out_specs=anywhere,
+        scratch_shapes=[
+            pltpu.VMEM((columns // LANE, LANE * planes, LANE), f32),
+            pltpu.VMEM(rhs.shape, bf16),
+            pltpu.SemaphoreType.DMA((chunks,)),
+        ],
+        compiler_params=pltpu.CompilerParams(vmem_limit_bytes=16 * 1024 * 1024),
     )(order, sol)
     return jnp.transpose(result[None, None], (0, 1, 3, 2, 4))
 

time: 61.3 us -> 54.8 us (0.89)
  Pallas kernels: 61.1 us -> 54.6 us
    pallas_call x1, Pallas kernels: 55.1 us -> 51.6 us  [on_device(): pl.pallas_call(sweep_kernel, out_shape=pltpu.VMEM((planes, block, columns...]
    pallas_call x1, Pallas kernels: 6.02 us -> 3 us  [on_device(): pl.pallas_call(place_kernel, out_shape=jax.ShapeDtypeStruct(rhs.shape, bf...]
where the time goes in v3:
time: 54.8 us; the launch traced here: 54.6 us
  Pallas kernels  54.6 us (100%)
    pallas_call x1, Pallas kernels, on_device(): pl.pallas_call(sweep_kernel, out_shape=pltpu.VMEM((planes, block, columns...  51.6 us
    pallas_call x1, Pallas kernels, on_device(): pl.pallas_call(place_kernel, out_shape=jax.ShapeDtypeStruct(rhs.shape, bf...  3 us

profile of v3, /device:TPU:31, one launch (start us, length us, event | category | flops | bytes accessed | tf_op | source)
XLA Modules:
  0.0 54.6 jit_solution(6543457462503353002)
XLA Ops:
  0.0 0.0 copy-start
  0.0 51.6 %shard_map.64.sol = bf16[8,625,256]{2,1,0:T(8,128)(2,1)S(1)} custom-call(s32[8]{0:T(128)} %bitcast.14, s32[3,1,8]{2,1,0:T(1,128)} %bitcast.19, bf16[8,128,128]{2,1,0:T(8,128)(2,1)} %constant.2.clone.table_hbm, bf16[375,625]{1,0:T(8,128)(2,1)} %bitcast.18, bf16[625,8,256]{2,1,0:T(8,128)(2,1)} %bitcast.17, bf16[625,8,625]{2,1,0:T(8,128)(2,1)} %bitcast.16), custom_call_target="tpu_custom_call" | custom-call | tf_op jit(solution)/shard_map/pallas_call | solution.py:323
  51.6 0.0 copy-done
  51.6 3.0 %shard_map.65 = bf16[625,8,256]{2,1,0:T(8,128)(2,1)} custom-call(s32[8]{0:T(128)S(1)} %bitcast.15, bf16[8,625,256]{2,1,0:T(8,128)(2,1)S(1)} %shard_map.64.sol), custom_call_target="tpu_custom_call" | custom-call | tf_op jit(solution)/shard_map/pallas_call | solution.py:357
Async XLA Ops:
  0.0 51.6 %copy-start = (s32[1,1,8]{2,1,0:T(1,128)S(1)}, s32[1,1,8]{2,1,0:T(1,128)}, u32[]{:S(2)}) copy-start(s32[1,1,8]{2,1,0:T(1,128)} %param.9) | copy-start | bytes 100

commit v4 on v3

--- a/solution.py
+++ b/solution.py
@@ -14,7 +14,7 @@
 FACE = VARS * SQUARE
 BLOCK = FACE * NODES
 LANE = 128
-CHUNKS = 2
+CHUNKS = 1
 MESH = pl.DeviceIdType.MESH
 
 

time: 54.8 us -> 53.9 us (0.984)
  Pallas kernels: 54.6 us -> 53.7 us
    pallas_call x1, Pallas kernels: 51.6 us -> 50.7 us  [on_device(): pl.pallas_call(sweep_kernel, out_shape=pltpu.VMEM((planes, block, columns...]
where the time goes in v4:
time: 53.9 us; the launch traced here: 53.7 us
  Pallas kernels  53.7 us (100%)
    pallas_call x1, Pallas kernels, on_device(): pl.pallas_call(sweep_kernel, out_shape=pltpu.VMEM((planes, block, columns...  50.7 us
    pallas_call x1, Pallas kernels, on_device(): pl.pallas_call(place_kernel, out_shape=jax.ShapeDtypeStruct(rhs.shape, bf...  3 us

profile of v4, /device:TPU:31, one launch (start us, length us, event | category | flops | bytes accessed | tf_op | source)
XLA Modules:
  0.0 53.7 jit_solution(4550880114060611025)
XLA Ops:
  0.0 0.0 copy-start
  0.0 50.7 %shard_map.64.sol = bf16[8,625,256]{2,1,0:T(8,128)(2,1)S(1)} custom-call(s32[8]{0:T(128)} %bitcast.14, s32[3,1,8]{2,1,0:T(1,128)} %bitcast.19, bf16[8,128,128]{2,1,0:T(8,128)(2,1)} %constant.2.clone.table_hbm, bf16[375,625]{1,0:T(8,128)(2,1)} %bitcast.18, bf16[625,8,256]{2,1,0:T(8,128)(2,1)} %bitcast.17, bf16[625,8,625]{2,1,0:T(8,128)(2,1)} %bitcast.16), custom_call_target="tpu_custom_call" | custom-call | tf_op jit(solution)/shard_map/pallas_call | solution.py:323
  50.7 0.0 copy-done
  50.7 3.0 %shard_map.65 = bf16[625,8,256]{2,1,0:T(8,128)(2,1)} custom-call(s32[8]{0:T(128)S(1)} %bitcast.15, bf16[8,625,256]{2,1,0:T(8,128)(2,1)S(1)} %shard_map.64.sol), custom_call_target="tpu_custom_call" | custom-call | tf_op jit(solution)/shard_map/pallas_call | solution.py:357
Async XLA Ops:
  0.0 50.7 %copy-start = (s32[1,1,8]{2,1,0:T(1,128)S(1)}, s32[1,1,8]{2,1,0:T(1,128)}, u32[]{:S(2)}) copy-start(s32[1,1,8]{2,1,0:T(1,128)} %param.9) | copy-start | bytes 100
